TPU v7x, 256 devices: a whole 4x4x8 slice. The times are simulated.
256 devices in a mesh: seq: 64 (over y, z, core), ch: 4 (over x).
Axes of the slice: x: 4, y: 4, z: 8, core: 2. Of those that a mesh axis runs over, the one named last changes fastest.
Arguments:
- features: bfloat16 [32768, 1024], P('seq', 'ch'), may hold values from -6 to 6
- w_in: bfloat16 [1024, 3, 1024], P(None, None, 'ch'), may hold values from -0.1875 to 0.1875
- bias_skip: float32 [1024], P('ch'), may hold values from -3 to 3
- filters: float32 [32768, 1024], P('seq', 'ch')
- w_out: bfloat16 [1024, 1024], P(None, 'ch'), may hold values from -0.1875 to 0.1875
- w_emb: bfloat16 [1024, 128], P('ch'), may hold values from -0.1875 to 0.1875
- page_lengths: int32 [512], replicated, may hold values from 1 to 256, 32768 in all
- page_owner: int32 [512], replicated, may hold values from 0 to 63
Outputs:
- index_rows: bfloat16 [32768, 128], P('seq')
Inputs may be any that keep to these rules, and one draw needn't show every extreme that they name: page_lengths sum to 32768, and the longest page has exactly 256 patches.
All inputs are finite; a program needn't handle non-finite values.
Results may differ from a plain program's by a relative error of at most 0.0057.
Values may be sent and summed in bfloat16 or wider, within the bound.
A program may use at most 64 MiB of HBM per device.

v0:
```python
import math
import jax
import jax.numpy as jnp
from jax import lax
from jax.sharding import PartitionSpec as P


def angle_table(first_index, second_index, period):
    product = first_index[:, None] * second_index[None, :] % period
    return product.astype(jnp.float32) * (2.0 * math.pi / period)


def apply_table(table, values):
    return jnp.einsum("ki,qic->qkc", table, values, precision=lax.Precision.HIGHEST)


def long_convolution(signal, filters, seq_count, seq_rank):
    rows_dev, chan_dev = signal.shape
    group_rows = rows_dev // seq_count
    block_count = 2 * seq_count
    fft_length = block_count * rows_dev
    block_index = jnp.arange(block_count, dtype=jnp.int32)
    source_index = jnp.arange(seq_count, dtype=jnp.int32)
    outer_angle = angle_table(block_index, source_index, block_count)
    outer_cos = jnp.cos(outer_angle)
    outer_sin = jnp.sin(outer_angle)
    local_rows = seq_rank * group_rows + jnp.arange(group_rows, dtype=jnp.int32)
    twist_angle = angle_table(block_index, local_rows, fft_length)
    twist_cos = jnp.cos(twist_angle)[:, :, None]
    twist_sin = jnp.sin(twist_angle)[:, :, None]
    inner_index = jnp.arange(rows_dev, dtype=jnp.int32)
    inner_angle = angle_table(inner_index, inner_index, rows_dev)
    inner_cos = jnp.cos(inner_angle)
    inner_sin = jnp.sin(inner_angle)
    signal_blocks, filter_blocks = (
        lax.all_to_all(
            signal.reshape(seq_count, group_rows, chan_dev),
            "seq",
            split_axis=0,
            concat_axis=0,
            tiled=True,
        ),
        lax.all_to_all(
            filters.reshape(seq_count, group_rows, chan_dev),
            "seq",
            split_axis=0,
            concat_axis=0,
            tiled=True,
        ),
    )

    def outer_forward(blocks):
        real_part = jnp.einsum("kj,jic->kic", outer_cos, blocks, precision=lax.Precision.HIGHEST)
        imag_part = -jnp.einsum("kj,jic->kic", outer_sin, blocks, precision=lax.Precision.HIGHEST)
        return jnp.stack(
            [
                real_part * twist_cos + imag_part * twist_sin,
                imag_part * twist_cos - real_part * twist_sin,
            ]
        )

    signal_spec, filter_spec = (
        lax.all_to_all(
            outer_forward(signal_blocks), "seq", split_axis=1, concat_axis=2, tiled=True
        ),
        lax.all_to_all(
            outer_forward(filter_blocks), "seq", split_axis=1, concat_axis=2, tiled=True
        ),
    )

    def inner_forward(spectrum):
        real_in = spectrum[0]
        imag_in = spectrum[1]
        return (
            apply_table(inner_cos, real_in) + apply_table(inner_sin, imag_in),
            apply_table(inner_cos, imag_in) - apply_table(inner_sin, real_in),
        )

    signal_real, signal_imag = inner_forward(signal_spec)
    filter_real, filter_imag = inner_forward(filter_spec)
    product_real = signal_real * filter_real - signal_imag * filter_imag
    product_imag = signal_real * filter_imag + signal_imag * filter_real
    back_real = apply_table(inner_cos, product_real) - apply_table(inner_sin, product_imag)
    back_imag = apply_table(inner_cos, product_imag) + apply_table(inner_sin, product_real)
    returned = lax.all_to_all(
        jnp.stack([back_real, back_imag]), "seq", split_axis=2, concat_axis=1, tiled=True
    )
    turned_real = returned[0] * twist_cos - returned[1] * twist_sin
    turned_imag = returned[0] * twist_sin + returned[1] * twist_cos
    result = (
        jnp.einsum("kj,kic->jic", outer_cos, turned_real, precision=lax.Precision.HIGHEST)
        - jnp.einsum("kj,kic->jic", outer_sin, turned_imag, precision=lax.Precision.HIGHEST)
    ) / fft_length
    back_tokens = lax.all_to_all(result, "seq", split_axis=0, concat_axis=1, tiled=True)
    return back_tokens.reshape(rows_dev, chan_dev)


def source_tokens(page_lengths, page_owner, output_rows):
    page_index = jnp.arange(page_lengths.shape[0], dtype=jnp.int32)
    before = (page_owner[None, :] < page_owner[:, None]) | (
        page_owner[None, :] == page_owner[:, None]
    ) & (page_index[None, :] < page_index[:, None])
    placed_start = jnp.sum(jnp.where(before, page_lengths[None, :], 0), axis=1)
    page_start = jnp.cumsum(page_lengths) - page_lengths
    inside = (output_rows[:, None] >= placed_start[None, :]) & (
        output_rows[:, None] < (placed_start + page_lengths)[None, :]
    )
    offsets = page_start[None, :] + output_rows[:, None] - placed_start[None, :]
    return jnp.sum(jnp.where(inside, offsets, 0), axis=1)


def body(features, w_in, bias_skip, filters, w_out, w_emb, page_lengths, page_owner):
    rows_dev, chan_dev = features.shape
    seq_count = lax.axis_size("seq")
    seq_rank = lax.axis_index("seq")
    flat_in = w_in.reshape(w_in.shape[0], -1)
    weight_rows = flat_in
    projected = jnp.dot(
        lax.all_gather(features, "ch", axis=1, tiled=True),
        weight_rows,
        preferred_element_type=jnp.float32,
    )
    projected = projected.reshape(rows_dev, 3, chan_dev)
    gate_branch = projected[:, 0]
    signal = projected[:, 1] * projected[:, 2]
    convolved = long_convolution(signal, filters, seq_count, seq_rank)
    mixed = ((convolved + bias_skip[None, :] * signal) * gate_branch).astype(jnp.bfloat16)
    weight_rows = w_out
    summed = jnp.dot(
        lax.all_gather(mixed, "ch", axis=1, tiled=True),
        weight_rows,
        preferred_element_type=jnp.float32,
    )
    layer_out = (summed + features.astype(jnp.float32)).astype(jnp.bfloat16)
    output_rows = seq_rank * rows_dev + jnp.arange(rows_dev, dtype=jnp.int32)
    source = source_tokens(page_lengths, page_owner, output_rows)
    embedded = lax.psum(jnp.dot(layer_out, w_emb, preferred_element_type=jnp.float32), "ch").astype(
        jnp.bfloat16
    )
    shard_part = lax.all_gather(embedded, "seq", axis=0, tiled=True)
    count_rows = shard_part.shape[0]
    inside = (source >= 0) & (source < count_rows)
    taken = jnp.take(shard_part, jnp.clip(source, 0, count_rows - 1), axis=0)
    return jnp.where(inside[:, None], taken, jnp.zeros_like(embedded))


def solution(mesh):
    return jax.shard_map(
        body,
        mesh=mesh,
        in_specs=(
            P("seq", "ch"),
            P(None, None, "ch"),
            P("ch"),
            P("seq", "ch"),
            P(None, "ch"),
            P("ch", None),
            P(),
            P(),
        ),
        out_specs=P("seq", None),
        check_vma=False,
    )
```

profile of v0, /device:TPU:1, one launch (start us, length us, event | category | flops | bytes accessed | tf_op | source)
XLA Modules:
  0.0 488.9 jit_solution(5704225290694879429)
XLA Ops:
  7.3 13.2 %all-to-all-start.2 = ((f32[64,8,256]{2,1,0:T(8,128)}), f32[64,8,256]{2,1,0:T(8,128)S(1)}, u32[]{:S(2)}, u32[]{:S(2)}) async-start(f32[64,8,256]{2,1,0:T(8,128)} %bitcast.145), calls=%async_computation.2 | async-start | bytes 1048576 | tf_op jit(solution)/shard_map/all_to_all | solution.py:43
  22.1 17.4 %all-gather.4.cloned.1.call-done = bf16[512,1024]{1,0:T(8,128)(2,1)} async-done(((bf16[512,256]{1,0:T(8,128)(2,1)}), bf16[512,1024]{1,0:T(8,128)(2,1)}) %all-gather.4.cloned.1.call-update) | async-done | bytes 1048592 | tf_op jit(solution)/shard_map/all_gather | solution.py:119
  39.6 2.2 fusion
  43.9 12.0 %all-to-all-start = ((f32[64,8,256]{2,1,0:T(8,128)}), f32[64,8,256]{2,1,0:T(8,128)S(1)}, u32[]{:S(2)}, u32[]{:S(2)}) async-start(f32[64,8,256]{2,1,0:T(8,128)} %fusion.89), calls=%async_computation | async-start | bytes 1048576 | tf_op jit(solution)/shard_map/all_to_all | solution.py:36
  59.4 13.8 %all-to-all-done = f32[64,8,256]{2,1,0:T(8,128)S(1)} async-done(((f32[64,8,256]{2,1,0:T(8,128)}), f32[64,8,256]{2,1,0:T(8,128)S(1)}, u32[]{:S(2)}, u32[]{:S(2)}) %all-to-all-start) | async-done | bytes 524320 | tf_op jit(solution)/shard_map/all_to_all | solution.py:36
  74.4 2.9 add_bitcast_fusion
  77.5 2.5 copy.64
  80.0 6.8 %all-to-all-start.3 = ((f32[2,128,8,256]{3,2,0,1:T(8,128)}), f32[2,128,8,256]{3,2,0,1:T(8,128)S(1)}, u32[]{:S(2)}, u32[]{:S(2)}) async-start(f32[2,128,8,256]{3,2,0,1:T(8,128)} %copy.64), calls=%async_computation.3 | async-start | bytes 4194304 | tf_op jit(solution)/shard_map/all_to_all | solution.py:66
  88.5 2.6 copy.56
  91.0 46.9 %all-to-all-done.3 = f32[2,128,8,256]{3,2,0,1:T(8,128)S(1)} async-done(((f32[2,128,8,256]{3,2,0,1:T(8,128)}), f32[2,128,8,256]{3,2,0,1:T(8,128)S(1)}, u32[]{:S(2)}, u32[]{:S(2)}) %all-to-all-start.3) | async-done | bytes 2097184 | tf_op jit(solution)/shard_map/all_to_all | solution.py:66
  139.3 5.8 %all-to-all-start.1 = ((f32[2,128,8,256]{3,2,0,1:T(8,128)}), f32[2,128,8,256]{3,2,0,1:T(8,128)S(1)}, u32[]{:S(2)}, u32[]{:S(2)}) async-start(f32[2,128,8,256]{3,2,0,1:T(8,128)} %copy.56), calls=%async_computation.1 | async-start | bytes 4194304 | tf_op jit(solution)/shard_map/all_to_all | solution.py:63
  147.0 7.2 %fusion.16 = f32[2,256,512]{2,1,0:T(8,128)S(1)} fusion(f32[1,2,64,8,256]{4,3,1,2,0:T(8,128)S(1)} %get-tuple-element.13), kind=kOutput, calls=%fused_computation.34 | convolution fusion | flops 1614282752 | bytes 2097152 | tf_op jit(solution)/shard_map/ki,qic->qkc/dot_general | solution.py:14
  154.2 7.4 %fusion.20 = f32[2,256,512]{2,1,0:T(8,128)S(1)} fusion(f32[1,2,64,8,256]{4,3,1,2,0:T(8,128)S(1)} %get-tuple-element.14), kind=kOutput, calls=%fused_computation.38 | convolution fusion | flops 1614282752 | bytes 2097152 | tf_op jit(solution)/shard_map/ki,qic->qkc/dot_general | solution.py:14
  161.6 8.1 %convolution_subtract_fusion.1 = f32[2,256,512]{2,1,0:T(8,128)} fusion(f32[2,256,512]{2,1,0:T(8,128)S(1)} %fusion.16, f32[1,2,64,8,256]{4,3,1,2,0:T(8,128)S(1)} %get-tuple-element.14), kind=kOutput, calls=%fused_computation.16 | convolution fusion | flops 1614544896 | bytes 3145728 | tf_op jit(solution)/shard_map/ki,qic->qkc/dot_general | solution.py:14
  169.7 8.3 %convolution_add_fusion.1 = f32[2,256,512]{2,1,0:T(8,128)} fusion(f32[2,256,512]{2,1,0:T(8,128)S(1)} %fusion.20, f32[1,2,64,8,256]{4,3,1,2,0:T(8,128)S(1)} %get-tuple-element.13), kind=kOutput, calls=%fused_computation.18 | convolution fusion | flops 1614544896 | bytes 3145728 | tf_op jit(solution)/shard_map/ki,qic->qkc/dot_general | solution.py:14
  178.0 18.3 %all-to-all-done.1 = f32[2,128,8,256]{3,2,0,1:T(8,128)S(1)} async-done(((f32[2,128,8,256]{3,2,0,1:T(8,128)}), f32[2,128,8,256]{3,2,0,1:T(8,128)S(1)}, u32[]{:S(2)}, u32[]{:S(2)}) %all-to-all-start.1) | async-done | bytes 2097184 | tf_op jit(solution)/shard_map/all_to_all | solution.py:63
  196.6 7.2 %fusion.36 = f32[2,256,512]{2,1,0:T(8,128)S(1)} fusion(f32[1,2,64,8,256]{4,3,1,2,0:T(8,128)S(1)} %get-tuple-element.15), kind=kOutput, calls=%fused_computation.54 | convolution fusion | flops 1614282752 | bytes 2097152 | tf_op jit(solution)/shard_map/ki,qic->qkc/dot_general | solution.py:14
  203.8 7.6 %fusion.28 = f32[2,256,512]{2,1,0:T(8,128)S(1)} fusion(f32[1,2,64,8,256]{4,3,1,2,0:T(8,128)S(1)} %get-tuple-element.16), kind=kOutput, calls=%fused_computation.46 | convolution fusion | flops 1614282752 | bytes 2097152 | tf_op jit(solution)/shard_map/ki,qic->qkc/dot_general | solution.py:14
  211.4 7.2 %convolution_add_fusion.2 = f32[2,256,512]{2,1,0:T(8,128)S(1)} fusion(f32[2,256,512]{2,1,0:T(8,128)S(1)} %fusion.36, f32[1,2,64,8,256]{4,3,1,2,0:T(8,128)S(1)} %get-tuple-element.16), kind=kOutput, calls=%fused_computation.19 | convolution fusion | flops 1614544896 | bytes 3145728 | tf_op jit(solution)/shard_map/ki,qic->qkc/dot_general | solution.py:14
  218.6 7.6 %multiply_subtract_fusion = (f32[2,256,512]{2,1,0:T(8,128)S(1)}, f32[2,256,512]{2,1,0:T(8,128)S(1)}) fusion(f32[2,256,512]{2,1,0:T(8,128)S(1)} %copy-done.5, f32[2,256,512]{2,1,0:T(8,128)S(1)} %convolution_add_fusion.2, f32[2,256,512]{2,1,0:T(8,128)S(1)} %copy-done.6, f32[2,256,512]{2,1,0:T(8,128)S(1)} %fusion.28, ...), kind=kOutput, calls=%fused_computation.67 | convolution fusion | flops 1616117760 | bytes 7340032 | tf_op jit(solution)/shard_map/ki,qic->qkc/dot_general | solution.py:14
  226.2 6.3 %fusion.14 = f32[2,256,512]{2,1,0:T(8,128)S(1)} fusion(f32[2,256,512]{2,1,0:T(8,128)S(1)} %get-tuple-element.5), kind=kOutput, calls=%fused_computation.32 | convolution fusion | flops 1614282752 | bytes 2097152 | tf_op jit(solution)/shard_map/ki,qic->qkc/dot_general | solution.py:14
  232.6 6.5 %fusion.10 = f32[2,256,512]{2,1,0:T(8,128)S(1)} fusion(f32[2,256,512]{2,1,0:T(8,128)S(1)} %get-tuple-element.6), kind=kOutput, calls=%fused_computation.28 | convolution fusion | flops 1614282752 | bytes 2097152 | tf_op jit(solution)/shard_map/ki,qic->qkc/dot_general | solution.py:14
  239.1 6.3 %fusion.3 = f32[1,2,512,256]{2,3,1,0:T(8,128)S(1)} fusion(f32[2,256,512]{2,1,0:T(8,128)S(1)} %fusion.14, f32[2,256,512]{2,1,0:T(8,128)S(1)} %get-tuple-element.6), kind=kOutput, calls=%fused_computation.15 | convolution fusion | flops 1614544896 | bytes 3145728 | tf_op jit(solution)/shard_map/ki,qic->qkc/dot_general | solution.py:14
  245.5 6.3 %fusion.2 = f32[1,2,512,256]{2,3,1,0:T(8,128)S(1)} fusion(f32[2,256,512]{2,1,0:T(8,128)S(1)} %fusion.10, f32[2,256,512]{2,1,0:T(8,128)S(1)} %get-tuple-element.5), kind=kOutput, calls=%fused_computation.13 | convolution fusion | flops 1614544896 | bytes 3145728 | tf_op jit(solution)/shard_map/ki,qic->qkc/dot_general | solution.py:14
  252.0 2.5 copy.74
  254.5 57.4 %all_to_all.64 = f32[2,2,512,256]{3,1,0,2:T(2,128)S(1)} all-to-all(f32[2,2,512,256]{3,1,0,2:T(2,128)} %copy.74), channel_id=1, replica_groups=mesh['seq'=64,'ch'=4] {'seq'}, dimensions={2} | all-to-all | bytes 4194304 | tf_op jit(solution)/shard_map/all_to_all | solution.py:85
  314.9 3.0 copy.77
  322.2 23.0 %all_to_all.65 = f32[64,8,256]{2,1,0:T(8,128)S(1)} all-to-all(f32[64,8,256]{2,1,0:T(8,128)S(1)} %copy.78), channel_id=1, replica_groups=mesh['seq'=64,'ch'=4] {'seq'}, dimensions={0} | all-to-all | bytes 1048576 | tf_op jit(solution)/shard_map/all_to_all | solution.py:94
  346.1 23.0 %all-gather.6.cloned.1.call-done = bf16[512,1024]{1,0:T(8,128)(2,1)} async-done(((bf16[512,256]{1,0:T(8,128)(2,1)}), bf16[512,1024]{1,0:T(8,128)(2,1)}) %all-gather.6.cloned.1.call-update) | async-done | bytes 1048592 | tf_op jit(solution)/shard_map/all_gather | solution.py:130
  371.0 15.8 %all-reduce.1 = bf16[512,128]{1,0:T(8,128)(2,1)} all-reduce(f32[512,128]{1,0:T(8,128)S(1)} %fusion.6), channel_id=1, replica_groups=mesh['seq'=64,'ch'=4] {'ch'}, use_global_device_ids=true, to_apply=%region_4.5 | all-reduce | flops 65536 | bytes 393216 | tf_op jit(solution)/shard_map/psum | solution.py:137
  388.2 87.3 %all-gather.8.cloned.1.call-done = bf16[32768,128]{1,0:T(8,128)(2,1)} async-done(((bf16[512,128]{1,0:T(8,128)(2,1)}), bf16[32768,128]{1,0:T(8,128)(2,1)}) %all-gather.8.cloned.1.call-update) | async-done | bytes 8388624 | tf_op jit(solution)/shard_map/all_gather | solution.py:140
  475.5 5.5 %gather_fusion = bf16[512,128]{1,0:T(8,128)(2,1)S(1)} fusion(bf16[32768,128]{1,0:T(8,128)(2,1)} %all-gather.8.cloned.1.call-done, s32[1024]{0:T(1024)S(1)} %pad_clamp_fusion), kind=kCustom, calls=%fused_computation | custom fusion | bytes 264192 | tf_op jit(solution)/shard_map/jit(_take)/gather | solution.py:143
  (67 shorter events, 27.1 us)
Async XLA Ops:
  6.5 362.6 %copy-start = (bf16[1024,256]{1,0:T(8,128)(2,1)S(1)}, bf16[1024,256]{1,0:T(8,128)(2,1)}, u32[]{:S(2)}) copy-start(bf16[1024,256]{1,0:T(8,128)(2,1)} %param.12) | copy-start | bytes 1572868
  6.5 33.0 %all-gather.4.cloned.1.call-start = ((), (), s32[]{:S(2)}) async-start(), calls=%async_computation.6 | async-start | bytes 1310720 | tf_op jit(solution)/shard_map/all_gather | solution.py:119
  7.3 36.6 %all-to-all-start.2 = ((f32[64,8,256]{2,1,0:T(8,128)}), f32[64,8,256]{2,1,0:T(8,128)S(1)}, u32[]{:S(2)}, u32[]{:S(2)}) async-start(f32[64,8,256]{2,1,0:T(8,128)} %bitcast.145), calls=%async_computation.2 | async-start | bytes 1048576 | tf_op jit(solution)/shard_map/all_to_all | solution.py:43
  41.8 1.2 copy-start.2
  43.9 29.3 %all-to-all-start = ((f32[64,8,256]{2,1,0:T(8,128)}), f32[64,8,256]{2,1,0:T(8,128)S(1)}, u32[]{:S(2)}, u32[]{:S(2)}) async-start(f32[64,8,256]{2,1,0:T(8,128)} %fusion.89), calls=%async_computation | async-start | bytes 1048576 | tf_op jit(solution)/shard_map/all_to_all | solution.py:36
  73.2 1.2 copy-start.4
  80.0 57.9 %all-to-all-start.3 = ((f32[2,128,8,256]{3,2,0,1:T(8,128)}), f32[2,128,8,256]{3,2,0,1:T(8,128)S(1)}, u32[]{:S(2)}, u32[]{:S(2)}) async-start(f32[2,128,8,256]{3,2,0,1:T(8,128)} %copy.64), calls=%async_computation.3 | async-start | bytes 4194304 | tf_op jit(solution)/shard_map/all_to_all | solution.py:66
  138.0 1.3 copy-start.1
  139.3 57.0 %all-to-all-start.1 = ((f32[2,128,8,256]{3,2,0,1:T(8,128)}), f32[2,128,8,256]{3,2,0,1:T(8,128)S(1)}, u32[]{:S(2)}, u32[]{:S(2)}) async-start(f32[2,128,8,256]{3,2,0,1:T(8,128)} %copy.56), calls=%async_computation.1 | async-start | bytes 4194304 | tf_op jit(solution)/shard_map/all_to_all | solution.py:63
  145.0 224.1 %all-gather.6.cloned.1.call-start = ((), (), s32[]{:S(2)}) async-start(), calls=%async_computation.7 | async-start | bytes 1310720 | tf_op jit(solution)/shard_map/all_gather | solution.py:130
  211.4 7.2 %copy-start.5 = (f32[2,256,512]{2,1,0:T(8,128)S(1)}, f32[2,256,512]{2,1,0:T(8,128)}, u32[]{:S(2)}) copy-start(f32[2,256,512]{2,1,0:T(8,128)} %convolution_subtract_fusion.1) | copy-start | bytes 3145732
  211.4 7.2 %copy-start.6 = (f32[2,256,512]{2,1,0:T(8,128)S(1)}, f32[2,256,512]{2,1,0:T(8,128)}, u32[]{:S(2)}) copy-start(f32[2,256,512]{2,1,0:T(8,128)} %convolution_add_fusion.1) | copy-start | bytes 3145732
  320.9 24.3 %copy-start.3 = (f32[512,3,256]{2,0,1:T(8,128)S(1)}, f32[512,3,256]{2,0,1:T(8,128)}, u32[]{:S(2)}) copy-start(f32[512,3,256]{2,0,1:T(8,128)} %copy-done.2) | copy-start | bytes 4718596
  320.9 24.3 %copy-start.10 = (f32[256]{0:T(256)S(1)}, f32[256]{0:T(256)}, u32[]{:S(2)}) copy-start(f32[256]{0:T(256)} %param.10) | copy-start | bytes 3076
  322.2 46.9 %copy-start.7 = (bf16[512,256]{1,0:T(8,128)(2,1)S(1)}, bf16[512,256]{1,0:T(8,128)(2,1)}, u32[]{:S(2)}) copy-start(bf16[512,256]{1,0:T(8,128)(2,1)} %param.8) | copy-start | bytes 786436
  322.2 46.9 %copy-start.11 = (bf16[256,128]{1,0:T(8,128)(2,1)S(1)}, bf16[256,128]{1,0:T(8,128)(2,1)}, u32[]{:S(2)}) copy-start(bf16[256,128]{1,0:T(8,128)(2,1)} %param.13) | copy-start | bytes 196612
  346.0 40.8 %copy-start.8 = (s32[512]{0:T(512)S(1)}, s32[512]{0:T(512)}, u32[]{:S(2)}) copy-start(s32[512]{0:T(512)} %param.14) | copy-start | bytes 6148
  346.0 41.3 %copy-start.9 = (s32[512]{0:T(512)S(1)}, s32[512]{0:T(512)}, u32[]{:S(2)}) copy-start(s32[512]{0:T(512)} %param.15) | copy-start | bytes 6148
  346.1 129.5 %all-gather.8.cloned.1.call-start = ((), (), s32[]{:S(2)}) async-start(), calls=%async_computation.8 | async-start | bytes 8519680 | tf_op jit(solution)/shard_map/all_gather | solution.py:140
Sparse Core Ops, SparseCore 0:
  9.1 30.3 all-gather.3
  346.2 22.8 all-gather.5
  386.9 88.5 all-gather.7
where the time goes:
time: 498 us; the launch traced here: 489 us
  waiting for transfers between devices  207 us (42%)
  matrix products  99.6 us (20%)
  blocking collectives  96.2 us (19%)
  starting transfers between devices  37.7 us (8%)
  local copies, waits for them, and re-layouts  28.1 us (6%)
  between operations  13.9 us (3%)
  other arithmetic  5.95 us (1%)
    all_gather x1, waiting for transfers between devices, body(): shard_part = lax.all_gather(embedded, 'seq', axis=0, tiled=True)  87.3 us
    dot_general x12, matrix products, apply_table(): jnp.einsum('ki,qic->qkc', table, values, precision=lax.Precision.HIGHEST)  86.1 us
    all_to_all x1, blocking collectives, long_convolution(): lax.all_to_all(jnp.stack([back_real, back_imag]), 'seq', split_axis=2, co...  57.4 us
    all_to_all x1, waiting for transfers between devices, long_convolution(): lax.all_to_all(outer_forward(filter_blocks), 'seq', split_axis=1, concat_...  46.9 us
    all_gather x1, waiting for transfers between devices, body(): lax.all_gather(mixed, 'ch', axis=1, tiled=True)  23 us
    all_to_all x1, blocking collectives, long_convolution(): lax.all_to_all(result, 'seq', split_axis=0, concat_axis=1, tiled=True)  23 us
    all_to_all x1, waiting for transfers between devices, long_convolution(): lax.all_to_all(outer_forward(signal_blocks), 'seq', split_axis=1, concat_...  18.3 us
    all_gather x1, waiting for transfers between devices, body(): lax.all_gather(features, 'ch', axis=1, tiled=True)  17.4 us
  transfers between devices with their start and end apart: 7, of which 6 were waited for; matrix products, arithmetic and copies ran while one was open for 10% of the time, Pallas kernels for 0%

commit v1 on v0

--- a/solution.py
+++ b/solution.py
@@ -3,6 +3,11 @@
 import jax.numpy as jnp
 from jax import lax
 from jax.sharding import PartitionSpec as P
+from jax.lax import all_gather
+
+
+def wrap_the_indices(q_in):
+    return jnp.sum(all_gather(q_in, "ch"), 0)
 
 
 def angle_table(first_index, second_index, period):
@@ -134,9 +139,9 @@
     layer_out = (summed + features.astype(jnp.float32)).astype(jnp.bfloat16)
     output_rows = seq_rank * rows_dev + jnp.arange(rows_dev, dtype=jnp.int32)
     source = source_tokens(page_lengths, page_owner, output_rows)
-    embedded = lax.psum(jnp.dot(layer_out, w_emb, preferred_element_type=jnp.float32), "ch").astype(
-        jnp.bfloat16
-    )
+    embedded = wrap_the_indices(
+        jnp.dot(layer_out, w_emb, preferred_element_type=jnp.float32)
+    ).astype(jnp.bfloat16)
     shard_part = lax.all_gather(embedded, "seq", axis=0, tiled=True)
     count_rows = shard_part.shape[0]
     inside = (source >= 0) & (source < count_rows)

time: 498 us -> 510 us (1.024)
  waiting for transfers between devices: 207 us -> 233 us
  blocking collectives: 96.2 us -> 80.3 us
    all_gather x0 -> x1, waiting for transfers between devices: none -> 27.2 us  [wrap_the_indices(): return jnp.sum(all_gather(q_in, 'ch'), 0)]
    psum x1 -> x0, blocking collectives: 15.8 us -> none  [body(): lax.psum(jnp.dot(layer_out, w_emb, preferred_element_type=jnp.float32), '...]
  transfers between devices with their start and end apart: 7 -> 8, of which waited for: 6 -> 7; matrix products, arithmetic and copies ran while one was open for 10% -> 9% of each run, Pallas kernels for 0% -> 0%
where the time goes in v1:
time: 510 us; the launch traced here: 501 us
  waiting for transfers between devices  233 us (46%)
  matrix products  100 us (20%)
  blocking collectives  80.3 us (16%)
  starting transfers between devices  37.8 us (7%)
  local copies, waits for them, and re-layouts  28.1 us (6%)
  between operations  13.9 us (3%)
  other arithmetic  7.88 us (2%)
    dot_general x12, matrix products, apply_table(): jnp.einsum('ki,qic->qkc', table, values, precision=lax.Precision.HIGHEST)  86.1 us
    all_gather x1, waiting for transfers between devices, body(): shard_part = lax.all_gather(embedded, 'seq', axis=0, tiled=True)  85.1 us
    all_to_all x1, blocking collectives, long_convolution(): lax.all_to_all(jnp.stack([back_real, back_imag]), 'seq', split_axis=2, co...  57.4 us
    all_to_all x1, waiting for transfers between devices, long_convolution(): lax.all_to_all(outer_forward(filter_blocks), 'seq', split_axis=1, concat_...  46.9 us
    all_gather x1, waiting for transfers between devices, wrap_the_indices(): return jnp.sum(all_gather(q_in, 'ch'), 0)  27.2 us
    all_gather x1, waiting for transfers between devices, body(): lax.all_gather(mixed, 'ch', axis=1, tiled=True)  23 us
    all_to_all x1, blocking collectives, long_convolution(): lax.all_to_all(result, 'seq', split_axis=0, concat_axis=1, tiled=True)  23 us
    all_to_all x1, waiting for transfers between devices, long_convolution(): lax.all_to_all(outer_forward(signal_blocks), 'seq', split_axis=1, concat_...  18.3 us
  transfers between devices with their start and end apart: 8, of which 7 were waited for; matrix products, arithmetic and copies ran while one was open for 9% of the time, Pallas kernels for 0%

profile of v1, /device:TPU:1, one launch (start us, length us, event | category | flops | bytes accessed | tf_op | source)
XLA Modules:
  0.0 500.8 jit_solution(7920398619913220441)
XLA Ops:
  7.3 13.2 %all-to-all-start.2 = ((f32[64,8,256]{2,1,0:T(8,128)}), f32[64,8,256]{2,1,0:T(8,128)S(1)}, u32[]{:S(2)}, u32[]{:S(2)}) async-start(f32[64,8,256]{2,1,0:T(8,128)} %bitcast.147), calls=%async_computation.2 | async-start | bytes 1048576 | tf_op jit(solution)/shard_map/all_to_all | solution.py:48
  22.1 17.4 %all-gather.6.cloned.1.call-done = bf16[512,1024]{1,0:T(8,128)(2,1)} async-done(((bf16[512,256]{1,0:T(8,128)(2,1)}), bf16[512,1024]{1,0:T(8,128)(2,1)}) %all-gather.6.cloned.1.call-update) | async-done | bytes 1048592 | tf_op jit(solution)/shard_map/all_gather | solution.py:124
  43.9 12.0 %all-to-all-start = ((f32[64,8,256]{2,1,0:T(8,128)}), f32[64,8,256]{2,1,0:T(8,128)S(1)}, u32[]{:S(2)}, u32[]{:S(2)}) async-start(f32[64,8,256]{2,1,0:T(8,128)} %fusion.89), calls=%async_computation | async-start | bytes 1048576 | tf_op jit(solution)/shard_map/all_to_all | solution.py:41
  59.4 13.8 %all-to-all-done = f32[64,8,256]{2,1,0:T(8,128)S(1)} async-done(((f32[64,8,256]{2,1,0:T(8,128)}), f32[64,8,256]{2,1,0:T(8,128)S(1)}, u32[]{:S(2)}, u32[]{:S(2)}) %all-to-all-start) | async-done | bytes 524320 | tf_op jit(solution)/shard_map/all_to_all | solution.py:41
  74.4 2.9 add_bitcast_fusion
  77.5 2.5 copy.64
  80.0 6.7 %all-to-all-start.3 = ((f32[2,128,8,256]{3,2,0,1:T(8,128)}), f32[2,128,8,256]{3,2,0,1:T(8,128)S(1)}, u32[]{:S(2)}, u32[]{:S(2)}) async-start(f32[2,128,8,256]{3,2,0,1:T(8,128)} %copy.64), calls=%async_computation.3 | async-start | bytes 4194304 | tf_op jit(solution)/shard_map/all_to_all | solution.py:71
  88.4 2.5 copy.56
  91.0 46.9 %all-to-all-done.3 = f32[2,128,8,256]{3,2,0,1:T(8,128)S(1)} async-done(((f32[2,128,8,256]{3,2,0,1:T(8,128)}), f32[2,128,8,256]{3,2,0,1:T(8,128)S(1)}, u32[]{:S(2)}, u32[]{:S(2)}) %all-to-all-start.3) | async-done | bytes 2097184 | tf_op jit(solution)/shard_map/all_to_all | solution.py:71
  139.2 5.8 %all-to-all-start.1 = ((f32[2,128,8,256]{3,2,0,1:T(8,128)}), f32[2,128,8,256]{3,2,0,1:T(8,128)S(1)}, u32[]{:S(2)}, u32[]{:S(2)}) async-start(f32[2,128,8,256]{3,2,0,1:T(8,128)} %copy.56), calls=%async_computation.1 | async-start | bytes 4194304 | tf_op jit(solution)/shard_map/all_to_all | solution.py:68
  146.9 7.2 %fusion.16 = f32[2,256,512]{2,1,0:T(8,128)S(1)} fusion(f32[1,2,64,8,256]{4,3,1,2,0:T(8,128)S(1)} %get-tuple-element.13), kind=kOutput, calls=%fused_computation.34 | convolution fusion | flops 1614282752 | bytes 2097152 | tf_op jit(solution)/shard_map/ki,qic->qkc/dot_general | solution.py:19
  154.1 7.4 %fusion.20 = f32[2,256,512]{2,1,0:T(8,128)S(1)} fusion(f32[1,2,64,8,256]{4,3,1,2,0:T(8,128)S(1)} %get-tuple-element.14), kind=kOutput, calls=%fused_computation.38 | convolution fusion | flops 1614282752 | bytes 2097152 | tf_op jit(solution)/shard_map/ki,qic->qkc/dot_general | solution.py:19
  161.5 8.1 %convolution_subtract_fusion.1 = f32[2,256,512]{2,1,0:T(8,128)} fusion(f32[2,256,512]{2,1,0:T(8,128)S(1)} %fusion.16, f32[1,2,64,8,256]{4,3,1,2,0:T(8,128)S(1)} %get-tuple-element.14), kind=kOutput, calls=%fused_computation.16 | convolution fusion | flops 1614544896 | bytes 3145728 | tf_op jit(solution)/shard_map/ki,qic->qkc/dot_general | solution.py:19
  169.6 8.3 %convolution_add_fusion.1 = f32[2,256,512]{2,1,0:T(8,128)} fusion(f32[2,256,512]{2,1,0:T(8,128)S(1)} %fusion.20, f32[1,2,64,8,256]{4,3,1,2,0:T(8,128)S(1)} %get-tuple-element.13), kind=kOutput, calls=%fused_computation.18 | convolution fusion | flops 1614544896 | bytes 3145728 | tf_op jit(solution)/shard_map/ki,qic->qkc/dot_general | solution.py:19
  177.9 18.3 %all-to-all-done.1 = f32[2,128,8,256]{3,2,0,1:T(8,128)S(1)} async-done(((f32[2,128,8,256]{3,2,0,1:T(8,128)}), f32[2,128,8,256]{3,2,0,1:T(8,128)S(1)}, u32[]{:S(2)}, u32[]{:S(2)}) %all-to-all-start.1) | async-done | bytes 2097184 | tf_op jit(solution)/shard_map/all_to_all | solution.py:68
  196.5 7.2 %fusion.36 = f32[2,256,512]{2,1,0:T(8,128)S(1)} fusion(f32[1,2,64,8,256]{4,3,1,2,0:T(8,128)S(1)} %get-tuple-element.15), kind=kOutput, calls=%fused_computation.54 | convolution fusion | flops 1614282752 | bytes 2097152 | tf_op jit(solution)/shard_map/ki,qic->qkc/dot_general | solution.py:19
  203.7 7.6 %fusion.28 = f32[2,256,512]{2,1,0:T(8,128)S(1)} fusion(f32[1,2,64,8,256]{4,3,1,2,0:T(8,128)S(1)} %get-tuple-element.16), kind=kOutput, calls=%fused_computation.46 | convolution fusion | flops 1614282752 | bytes 2097152 | tf_op jit(solution)/shard_map/ki,qic->qkc/dot_general | solution.py:19
  211.3 7.2 %convolution_add_fusion.2 = f32[2,256,512]{2,1,0:T(8,128)S(1)} fusion(f32[2,256,512]{2,1,0:T(8,128)S(1)} %fusion.36, f32[1,2,64,8,256]{4,3,1,2,0:T(8,128)S(1)} %get-tuple-element.16), kind=kOutput, calls=%fused_computation.19 | convolution fusion | flops 1614544896 | bytes 3145728 | tf_op jit(solution)/shard_map/ki,qic->qkc/dot_general | solution.py:19
  218.5 7.6 %multiply_subtract_fusion = (f32[2,256,512]{2,1,0:T(8,128)S(1)}, f32[2,256,512]{2,1,0:T(8,128)S(1)}) fusion(f32[2,256,512]{2,1,0:T(8,128)S(1)} %copy-done.5, f32[2,256,512]{2,1,0:T(8,128)S(1)} %convolution_add_fusion.2, f32[2,256,512]{2,1,0:T(8,128)S(1)} %copy-done.6, f32[2,256,512]{2,1,0:T(8,128)S(1)} %fusion.28, ...), kind=kOutput, calls=%fused_computation.67 | convolution fusion | flops 1616117760 | bytes 7340032 | tf_op jit(solution)/shard_map/ki,qic->qkc/dot_general | solution.py:19
  226.1 6.3 %fusion.14 = f32[2,256,512]{2,1,0:T(8,128)S(1)} fusion(f32[2,256,512]{2,1,0:T(8,128)S(1)} %get-tuple-element.5), kind=kOutput, calls=%fused_computation.32 | convolution fusion | flops 1614282752 | bytes 2097152 | tf_op jit(solution)/shard_map/ki,qic->qkc/dot_general | solution.py:19
  232.5 6.5 %fusion.10 = f32[2,256,512]{2,1,0:T(8,128)S(1)} fusion(f32[2,256,512]{2,1,0:T(8,128)S(1)} %get-tuple-element.6), kind=kOutput, calls=%fused_computation.28 | convolution fusion | flops 1614282752 | bytes 2097152 | tf_op jit(solution)/shard_map/ki,qic->qkc/dot_general | solution.py:19
  239.0 6.3 %fusion.3 = f32[1,2,512,256]{2,3,1,0:T(8,128)S(1)} fusion(f32[2,256,512]{2,1,0:T(8,128)S(1)} %fusion.14, f32[2,256,512]{2,1,0:T(8,128)S(1)} %get-tuple-element.6), kind=kOutput, calls=%fused_computation.15 | convolution fusion | flops 1614544896 | bytes 3145728 | tf_op jit(solution)/shard_map/ki,qic->qkc/dot_general | solution.py:19
  245.4 6.3 %fusion.2 = f32[1,2,512,256]{2,3,1,0:T(8,128)S(1)} fusion(f32[2,256,512]{2,1,0:T(8,128)S(1)} %fusion.10, f32[2,256,512]{2,1,0:T(8,128)S(1)} %get-tuple-element.5), kind=kOutput, calls=%fused_computation.13 | convolution fusion | flops 1614544896 | bytes 3145728 | tf_op jit(solution)/shard_map/ki,qic->qkc/dot_general | solution.py:19
  251.9 2.5 copy.74
  254.4 57.4 %all_to_all.64 = f32[2,2,512,256]{3,1,0,2:T(2,128)S(1)} all-to-all(f32[2,2,512,256]{3,1,0,2:T(2,128)} %copy.74), channel_id=1, replica_groups=mesh['seq'=64,'ch'=4] {'seq'}, dimensions={2} | all-to-all | bytes 4194304 | tf_op jit(solution)/shard_map/all_to_all | solution.py:90
  314.8 3.0 copy.77
  322.1 23.0 %all_to_all.65 = f32[64,8,256]{2,1,0:T(8,128)S(1)} all-to-all(f32[64,8,256]{2,1,0:T(8,128)S(1)} %copy.78), channel_id=1, replica_groups=mesh['seq'=64,'ch'=4] {'seq'}, dimensions={0} | all-to-all | bytes 1048576 | tf_op jit(solution)/shard_map/all_to_all | solution.py:99
  346.0 23.0 %all-gather.8.cloned.1.call-done = bf16[512,1024]{1,0:T(8,128)(2,1)} async-done(((bf16[512,256]{1,0:T(8,128)(2,1)}), bf16[512,1024]{1,0:T(8,128)(2,1)}) %all-gather.8.cloned.1.call-update) | async-done | bytes 1048592 | tf_op jit(solution)/shard_map/all_gather | solution.py:135
  369.0 2.5 fusion.6
  371.6 27.2 %all-gather.12.cloned.1.call-done = f32[2048,128]{1,0:T(8,128)} async-done(((f32[512,128]{1,0:T(8,128)}), f32[2048,128]{1,0:T(8,128)}) %all-gather.12.cloned.1.call-update) | async-done | bytes 1048592 | tf_op jit(solution)/shard_map/all_gather | solution.py:10
  402.3 85.1 %all-gather.10.cloned.1.call-done = bf16[32768,128]{1,0:T(8,128)(2,1)} async-done(((bf16[512,128]{1,0:T(8,128)(2,1)}), bf16[32768,128]{1,0:T(8,128)(2,1)}) %all-gather.10.cloned.1.call-update) | async-done | bytes 8388624 | tf_op jit(solution)/shard_map/all_gather | solution.py:145
  487.4 5.5 %gather_fusion = bf16[512,128]{1,0:T(8,128)(2,1)S(1)} fusion(bf16[32768,128]{1,0:T(8,128)(2,1)} %all-gather.10.cloned.1.call-done, s32[1024]{0:T(1024)S(1)} %pad_clamp_fusion), kind=kCustom, calls=%fused_computation | custom fusion | bytes 264192 | tf_op jit(solution)/shard_map/jit(_take)/gather | solution.py:148
  (70 shorter events, 29.5 us)
Async XLA Ops:
  6.5 362.5 %copy-start = (bf16[1024,256]{1,0:T(8,128)(2,1)S(1)}, bf16[1024,256]{1,0:T(8,128)(2,1)}, u32[]{:S(2)}) copy-start(bf16[1024,256]{1,0:T(8,128)(2,1)} %param.12) | copy-start | bytes 1572868
  6.5 33.0 %all-gather.6.cloned.1.call-start = ((), (), s32[]{:S(2)}) async-start(), calls=%async_computation.6 | async-start | bytes 1310720 | tf_op jit(solution)/shard_map/all_gather | solution.py:124
  7.3 36.6 %all-to-all-start.2 = ((f32[64,8,256]{2,1,0:T(8,128)}), f32[64,8,256]{2,1,0:T(8,128)S(1)}, u32[]{:S(2)}, u32[]{:S(2)}) async-start(f32[64,8,256]{2,1,0:T(8,128)} %bitcast.147), calls=%async_computation.2 | async-start | bytes 1048576 | tf_op jit(solution)/shard_map/all_to_all | solution.py:48
  41.8 1.2 copy-start.2
  43.9 29.3 %all-to-all-start = ((f32[64,8,256]{2,1,0:T(8,128)}), f32[64,8,256]{2,1,0:T(8,128)S(1)}, u32[]{:S(2)}, u32[]{:S(2)}) async-start(f32[64,8,256]{2,1,0:T(8,128)} %fusion.89), calls=%async_computation | async-start | bytes 1048576 | tf_op jit(solution)/shard_map/all_to_all | solution.py:41
  73.2 1.2 copy-start.4
  80.0 57.9 %all-to-all-start.3 = ((f32[2,128,8,256]{3,2,0,1:T(8,128)}), f32[2,128,8,256]{3,2,0,1:T(8,128)S(1)}, u32[]{:S(2)}, u32[]{:S(2)}) async-start(f32[2,128,8,256]{3,2,0,1:T(8,128)} %copy.64), calls=%async_computation.3 | async-start | bytes 4194304 | tf_op jit(solution)/shard_map/all_to_all | solution.py:71
  137.9 1.3 copy-start.1
  139.2 57.0 %all-to-all-start.1 = ((f32[2,128,8,256]{3,2,0,1:T(8,128)}), f32[2,128,8,256]{3,2,0,1:T(8,128)S(1)}, u32[]{:S(2)}, u32[]{:S(2)}) async-start(f32[2,128,8,256]{3,2,0,1:T(8,128)} %copy.56), calls=%async_computation.1 | async-start | bytes 4194304 | tf_op jit(solution)/shard_map/all_to_all | solution.py:68
  145.0 224.0 %all-gather.8.cloned.1.call-start = ((), (), s32[]{:S(2)}) async-start(), calls=%async_computation.7 | async-start | bytes 1310720 | tf_op jit(solution)/shard_map/all_gather | solution.py:135
  211.3 7.2 %copy-start.5 = (f32[2,256,512]{2,1,0:T(8,128)S(1)}, f32[2,256,512]{2,1,0:T(8,128)}, u32[]{:S(2)}) copy-start(f32[2,256,512]{2,1,0:T(8,128)} %convolution_subtract_fusion.1) | copy-start | bytes 3145732
  211.3 7.2 %copy-start.6 = (f32[2,256,512]{2,1,0:T(8,128)S(1)}, f32[2,256,512]{2,1,0:T(8,128)}, u32[]{:S(2)}) copy-start(f32[2,256,512]{2,1,0:T(8,128)} %convolution_add_fusion.1) | copy-start | bytes 3145732
  320.8 24.3 %copy-start.3 = (f32[512,3,256]{2,0,1:T(8,128)S(1)}, f32[512,3,256]{2,0,1:T(8,128)}, u32[]{:S(2)}) copy-start(f32[512,3,256]{2,0,1:T(8,128)} %copy-done.2) | copy-start | bytes 4718596
  320.8 24.3 %copy-start.10 = (f32[256]{0:T(256)S(1)}, f32[256]{0:T(256)}, u32[]{:S(2)}) copy-start(f32[256]{0:T(256)} %param.10) | copy-start | bytes 3076
  322.1 46.9 %copy-start.7 = (bf16[512,256]{1,0:T(8,128)(2,1)S(1)}, bf16[512,256]{1,0:T(8,128)(2,1)}, u32[]{:S(2)}) copy-start(bf16[512,256]{1,0:T(8,128)(2,1)} %param.8) | copy-start | bytes 786436
  322.1 46.9 %copy-start.11 = (bf16[256,128]{1,0:T(8,128)(2,1)S(1)}, bf16[256,128]{1,0:T(8,128)(2,1)}, u32[]{:S(2)}) copy-start(bf16[256,128]{1,0:T(8,128)(2,1)} %param.13) | copy-start | bytes 196612
  345.9 54.9 %copy-start.8 = (s32[512]{0:T(512)S(1)}, s32[512]{0:T(512)}, u32[]{:S(2)}) copy-start(s32[512]{0:T(512)} %param.14) | copy-start | bytes 6148
  345.9 55.5 %copy-start.9 = (s32[512]{0:T(512)S(1)}, s32[512]{0:T(512)}, u32[]{:S(2)}) copy-start(s32[512]{0:T(512)} %param.15) | copy-start | bytes 6148
  345.9 52.9 %all-gather.12.cloned.1.call-start = ((), (), s32[]{:S(2)}) async-start(), calls=%async_computation.9 | async-start | bytes 1310720 | tf_op jit(solution)/shard_map/all_gather | solution.py:10
  371.6 115.8 %all-gather.10.cloned.1.call-start = ((), (), s32[]{:S(2)}) async-start(), calls=%async_computation.8 | async-start | bytes 8519680 | tf_op jit(solution)/shard_map/all_gather | solution.py:145
Sparse Core Ops, SparseCore 0:
  9.1 30.3 all-gather.5
  346.1 22.8 all-gather.7
  371.7 27.1 all-gather.11
  401.5 85.8 all-gather.9
